TPU v7x, 32 devices: a whole 2x2x4 slice. The times are simulated.
32 devices in a mesh: dp: 4 (over x, core), fsdp: 8 (over z, y).
Axes of the slice: x: 2, y: 2, z: 4, core: 2. Of those that a mesh axis runs over, the one named last changes fastest.
Arguments:
- queries: bfloat16 [64, 128, 1280], P(('dp', 'fsdp')), may hold values from -100 to 100
- keys: bfloat16 [64, 128, 1280], P(('dp', 'fsdp')), may hold values from -100 to 100
- values: bfloat16 [64, 128, 1280], P(('dp', 'fsdp')), may hold values from -64 to 64
- block_len: int32 [64], P(('dp', 'fsdp')), may hold values from 0 to 128, as said below
- target: int32 [64], P(('dp', 'fsdp')), may hold values from 0 to 2, as said below
- cotangent: bfloat16 [32, 128, 1280], P(('dp', 'fsdp')), may hold values from -6 to 6
- out_weight: bfloat16 [1280, 1280], P('fsdp'), may hold values from -0.15625 to 0.15625
Outputs:
- embedding: bfloat16 [32, 128, 1280], P(('dp', 'fsdp'))
- weight_grad: float32 [1280, 1280], P('fsdp')
Inputs may be any that keep to these rules, and one draw needn't show every extreme that they name: `block_len`: 0 exactly in the empty slots, those with target 2; live blocks hold 1 to 128 patches; in every draw some device has all its slots live and full. `target`: t < 1: output slot t of the same device; 1 <= t < 2: output slot t - 1 of the next device along dp (wrapping), same fsdp index; t = 2: empty slot; live values are distinct within a device, every output slot receives exactly one block, and in every draw some device has all 2 slots live.
All inputs are finite; a program needn't handle non-finite values.
Results may differ from a plain program's by a relative error of at most 0.012.
Values may be sent and summed in bfloat16 or wider, within the bound.
A program may use at most 64 MiB of HBM per device.

v0:
```python
import jax
import jax.numpy as jnp
from jax import lax
from jax.sharding import PartitionSpec as P

HEADS = 16


def from_behind(shard, axis, by):
    size = lax.axis_size(axis)
    return lax.ppermute(shard, axis, [(i, (i + by) % size) for i in range(size)])


def attend(query, key_block, value_block, length):
    blocks, window, features = query.shape
    head_dim = features // HEADS
    shape = (blocks, window, HEADS, head_dim)
    query_heads = query.reshape(shape)
    key_heads = key_block.reshape(shape)
    value_heads = value_block.reshape(shape)
    scores = jnp.einsum(
        "bqhd,bkhd->bhqk", query_heads, key_heads, preferred_element_type=jnp.float32
    ) * head_dim ** (-0.5)
    position = jnp.arange(window, dtype=jnp.int32)
    usable = position[None, :] < length[:, None]
    scores = jnp.where(usable[:, None, None, :], scores, -1e30)
    highest = jnp.max(scores, axis=-1, keepdims=True)
    exponent = jnp.exp(scores - highest)
    attn_weights = (exponent / jnp.sum(exponent, axis=-1, keepdims=True)).astype(jnp.bfloat16)
    mixed_out = jnp.einsum(
        "bhqk,bkhd->bqhd", attn_weights, value_heads, preferred_element_type=jnp.float32
    )
    mixed_out = jnp.where(usable[:, :, None, None], mixed_out, 0.0)
    return mixed_out.reshape(blocks, window, features).astype(jnp.bfloat16)


def pack_slots(target, arrays):
    slot_count = target.shape[0]
    select_map = (target[None, :] == jnp.arange(slot_count, dtype=jnp.int32)[:, None]).astype(
        jnp.bfloat16
    )
    return tuple(
        (
            jnp.einsum(
                "ts,swd->twd", select_map, array_item, preferred_element_type=jnp.float32
            ).astype(jnp.bfloat16)
            for array_item in arrays
        )
    )


def local(queries, keys, values, block_len, target, cotangent, out_weight):
    own_slots = cotangent.shape[0]
    local_out = attend(queries, keys, values, block_len)
    out_pack = pack_slots(target, (local_out,))[0]
    arrived = from_behind(out_pack[own_slots:], "dp", 1)
    attended = out_pack[:own_slots] + arrived
    features = attended.shape[-1]
    flat_rows = attended.reshape(-1, features)
    row_total = flat_rows.shape[0]
    columns = flat_rows
    projected = jnp.dot(
        columns,
        lax.all_gather(out_weight, "fsdp", axis=0, tiled=True),
        preferred_element_type=jnp.float32,
    )
    embedding = projected.astype(jnp.bfloat16).reshape(attended.shape)
    cot_rows = cotangent.reshape(row_total, features)
    columns = flat_rows
    fsdp_summed = lax.psum_scatter(
        lax.dot_general(
            columns, cot_rows, (((0,), (0,)), ((), ())), preferred_element_type=jnp.float32
        ).astype(jnp.bfloat16),
        "fsdp",
        scatter_dimension=0,
        tiled=True,
    ).astype(jnp.float32)
    summed = lax.psum(fsdp_summed, "dp")
    squares = lax.psum(jnp.sum(summed * summed), "fsdp")
    norm_value = jnp.sqrt(squares + 1e-06)
    factor = jnp.minimum(1.0, float(features) / norm_value)
    return (embedding, summed * factor)


def solution(mesh):
    placed = (
        P(("dp", "fsdp"), None, None),
        P(("dp", "fsdp"), None, None),
        P(("dp", "fsdp"), None, None),
        P(("dp", "fsdp")),
        P(("dp", "fsdp")),
        P(("dp", "fsdp"), None, None),
        P("fsdp", None),
    )
    return jax.shard_map(
        local,
        mesh=mesh,
        in_specs=placed,
        out_specs=(P(("dp", "fsdp"), None, None), P("fsdp", None)),
        check_vma=False,
    )
```

profile of v0, /device:TPU:0, one launch (start us, length us, event | category | flops | bytes accessed | tf_op | source)
XLA Modules:
  0.0 201.7 jit_solution(7435030648020174563)
XLA Ops:
  7.2 0.0 reduce-scatter.2.cloned.1.call-start
  7.2 0.8 iota_compare_fusion
  8.0 1.4 copy.19
  9.5 1.4 copy.20
  10.9 0.3 copy.21
  11.3 2.3 %fusion.18 = (f32[2,16,128]{2,1,0:T(8,128)S(1)}, f32[2,16,128,128]{2,3,1,0:T(8,128)}) fusion(pred[2,128]{1,0:T(4,128)(4,1)S(1)} %iota_compare_fusion, bf16[2,128,16,80]{1,3,2,0:T(8,128)(2,1)S(1)} %bitcast.25, bf16[2,128,16,80]{1,3,2,0:T(8,128)(2,1)S(1)} %bitcast.26), kind=kOutput, calls=%fused_computation.29 | convolution fusion | flops 85983360 | bytes 3424512 | tf_op jit(solution)/shard_map/sub | solution.py:28
  13.6 2.1 %fusion.3 = bf16[2,16,128,80]{2,3,1,0:T(8,128)(2,1)S(1)} fusion(bf16[2,128,16,80]{1,3,2,0:T(8,128)(2,1)S(1)} %bitcast.24, f32[2,16,128,128]{2,3,1,0:T(8,128)} %get-tuple-element.3, f32[2,16,128]{2,1,0:T(8,128)S(1)} %get-tuple-element.2, pred[2,128]{1,0:T(4,128)(4,1)S(1)} %iota_compare_fusion), kind=kOutput, calls=%fused_computation.10 | convolution fusion | flops 85590016 | bytes 3424512 | tf_op jit(solution)/shard_map/bhqk,bkhd->bqhd/dot_general | solution.py:30
  15.8 1.0 copy.23
  16.7 0.8 convolution_convert_fusion.1
  17.6 0.7 slice.9
  18.3 0.5 collective-permute-start
  18.9 6.7 %collective-permute-done = bf16[1,128,1280]{2,1,0:T(8,128)(2,1)S(1)} collective-permute-done((bf16[1,128,1280]{2,1,0:T(8,128)(2,1)S(1)}, bf16[1,128,1280]{2,1,0:T(8,128)(2,1)S(1)}, u32[]{:S(2)}, u32[]{:S(2)}) %collective-permute-start) | collective-permute-done | bytes 327712 | tf_op jit(solution)/shard_map/ppermute | solution.py:11
  25.6 0.8 slice_add_fusion
  26.3 2.8 %convolution_convert_fusion = bf16[1280,1280]{1,0:T(8,128)(2,1)} fusion(bf16[1,128,1280]{2,1,0:T(8,128)(2,1)S(1)} %copy-done, bf16[1,128,1280]{2,0,1:T(2,128)(2,1)S(1)} %slice_add_fusion), kind=kOutput, calls=%fused_computation.1 | convolution fusion | flops 421068800 | bytes 3932160 | tf_op jit(solution)/shard_map/dot_general | solution.py:71
  29.1 0.0 reduce-scatter.2.cloned.1.call-update
  29.1 0.0 all-gather.2.cloned.1.call-start
  29.2 0.7 all-gather.2.cloned.1.call-update
  29.9 77.8 %reduce-scatter.2.cloned.1.call-done = bf16[160,1280]{1,0:T(8,128)(2,1)} async-done(((bf16[1280,1280]{1,0:T(8,128)(2,1)}), bf16[160,1280]{1,0:T(8,128)(2,1)}) %reduce-scatter.2.cloned.1.call-update) | async-done | bytes 409616 | tf_op jit(solution)/shard_map/reduce_scatter | solution.py:70
  107.7 20.2 %all-reduce.1 = f32[160,1280]{1,0:T(8,128)S(1)} all-reduce(bf16[160,1280]{1,0:T(8,128)(2,1)} %reduce-scatter.2.cloned.1.call-done), channel_id=1, replica_groups=mesh['dp'=4,'fsdp'=8] {'dp'}, use_global_device_ids=true, to_apply=%region_3.4 | all-reduce | flops 204800 | bytes 1228800 | tf_op jit(solution)/shard_map/psum | solution.py:78
  127.9 0.8 multiply_reduce_fusion
  128.7 41.6 %all-gather.2.cloned.1.call-done = bf16[1280,1280]{1,0:T(8,128)(2,1)} async-done(((bf16[160,1280]{1,0:T(8,128)(2,1)}), bf16[1280,1280]{1,0:T(8,128)(2,1)}) %all-gather.2.cloned.1.call-update) | async-done | bytes 3276816 | tf_op jit(solution)/shard_map/all_gather | solution.py:64
  170.3 3.3 %fusion.1 = bf16[1,128,1280]{2,1,0:T(8,128)(2,1)} fusion(bf16[1280,1280]{1,0:T(8,128)(2,1)} %all-gather.2.cloned.1.call-done, bf16[1,128,1280]{2,0,1:T(2,128)(2,1)S(1)} %slice_add_fusion), kind=kOutput, calls=%fused_computation.4 | convolution fusion | flops 419594240 | bytes 3932160 | tf_op jit(solution)/shard_map/dot_general | solution.py:62
  173.5 19.7 %psum.15 = f32[]{:T(128)} all-reduce(f32[]{:T(128)} %multiply_reduce_fusion), channel_id=1, replica_groups=mesh['dp'=4,'fsdp'=8] {'fsdp'}, use_global_device_ids=true, to_apply=%region_5.6 | all-reduce | flops 1 | bytes 8 | tf_op jit(solution)/shard_map/psum | solution.py:79
  194.0 0.9 broadcast_multiply_fusion
  (7 shorter events, 0.1 us)
Async XLA Ops:
  7.2 19.2 %copy-start = (bf16[1,128,1280]{2,1,0:T(8,128)(2,1)S(1)}, bf16[1,128,1280]{2,1,0:T(8,128)(2,1)}, u32[]{:S(2)}) copy-start(bf16[1,128,1280]{2,1,0:T(8,128)(2,1)} %param.12) | copy-start | bytes 983044
  7.2 3.7 %copy-start.1 = (bf16[2,128,1280]{2,1,0:T(8,128)(2,1)S(1)}, bf16[2,128,1280]{2,1,0:T(8,128)(2,1)}, u32[]{:S(2)}) copy-start(bf16[2,128,1280]{2,1,0:T(8,128)(2,1)} %param.9) | copy-start | bytes 1966084
  7.2 100.5 %reduce-scatter.2.cloned.1.call-start = ((), (), s32[]{:S(2)}) async-start(), calls=%async_computation.2 | async-start | bytes 3686400 | tf_op jit(solution)/shard_map/reduce_scatter | solution.py:70
  13.6 3.1 %copy-start.2 = (s32[2]{0:T(128)S(1)}, s32[2]{0:T(128)}, u32[]{:S(2)}) copy-start(s32[2]{0:T(128)} %param.11) | copy-start | bytes 28
  18.3 7.2 %collective-permute-start = (bf16[1,128,1280]{2,1,0:T(8,128)(2,1)S(1)}, bf16[1,128,1280]{2,1,0:T(8,128)(2,1)S(1)}, u32[]{:S(2)}, u32[]{:S(2)}) collective-permute-start(bf16[1,128,1280]{2,1,0:T(8,128)(2,1)S(1)} %copy.24), channel_id=1, source_target_pairs={{0,8},{8,16},{16,24},{24,0},{1,9},{9,17},{17,25},{25,1},{2,10},{10... | collective-permute-start | bytes 983048 | tf_op jit(solution)/shard_map/ppermute | solution.py:11
  29.1 141.2 %all-gather.2.cloned.1.call-start = ((), (), s32[]{:S(2)}) async-start(), calls=%async_computation.1 | async-start | bytes 3686400 | tf_op jit(solution)/shard_map/all_gather | solution.py:64
Sparse Core Ops, SparseCore 0:
  29.2 78.3 reduce-scatter.1
  109.8 60.3 all-gather.1
where the time goes:
time: 202 us
  waiting for transfers between devices  127 us (63%)
  blocking collectives  40 us (20%)
  between operations  14.8 us (7%)
  matrix products  11.3 us (6%)
  local copies, waits for them, and re-layouts  4.93 us (2%)
  other arithmetic  3.32 us (2%)
    reduce_scatter x1, waiting for transfers between devices, local(): lax.psum_scatter(lax.dot_general(columns, cot_rows, (((0,), (0,)), ((), (...  77.8 us
    all_gather x1, waiting for transfers between devices, local(): lax.all_gather(out_weight, 'fsdp', axis=0, tiled=True)  41.6 us
    psum x1, blocking collectives, local(): summed = lax.psum(fsdp_summed, 'dp')  20.2 us
    psum x1, blocking collectives, local(): squares = lax.psum(jnp.sum(summed * summed), 'fsdp')  19.7 us
    ppermute x1, waiting for transfers between devices, from_behind(): lax.ppermute(shard, axis, [(i, (i + by) % size) for i in range(size)])  6.68 us
  transfers between devices with their start and end apart: 3, of which 3 were waited for; matrix products, arithmetic and copies ran while one was open for 0% of the time, Pallas kernels for 0%

commit v1 on v0

--- a/solution.py
+++ b/solution.py
@@ -50,6 +50,21 @@
 
 
 def local(queries, keys, values, block_len, target, cotangent, out_weight):
+
+    def finish_views_on_mesh(state, d_out):
+        everything = jax.lax.axis_size("fsdp")
+        big = jax.lax.axis_index("fsdp")
+        state_next, last, field_out = (everything, big, state.shape[d_out])
+        z2, z = (state, 1)
+        while z < state_next:
+            seen = []
+            for ii in range(state_next):
+                seen.append((ii, (ii - z) % state_next))
+            side_arr = jax.lax.ppermute(z2, "fsdp", seen)
+            z2 = jnp.concatenate([z2, side_arr], d_out)
+            z = 2 * z
+        return jnp.roll(z2, last * field_out, d_out)
+
     own_slots = cotangent.shape[0]
     local_out = attend(queries, keys, values, block_len)
     out_pack = pack_slots(target, (local_out,))[0]
@@ -60,9 +75,7 @@
     row_total = flat_rows.shape[0]
     columns = flat_rows
     projected = jnp.dot(
-        columns,
-        lax.all_gather(out_weight, "fsdp", axis=0, tiled=True),
-        preferred_element_type=jnp.float32,
+        columns, finish_views_on_mesh(out_weight, 0), preferred_element_type=jnp.float32
     )
     embedding = projected.astype(jnp.bfloat16).reshape(attended.shape)
     cot_rows = cotangent.reshape(row_total, features)

time: 202 us -> 234 us (1.16)
  local copies, waits for them, and re-layouts: 4.93 us -> 16.5 us
  waiting for transfers between devices: 127 us -> 138 us
  starting transfers between devices: 0.62 us -> 6.06 us
    ppermute x0 -> x3, waiting for transfers between devices: none -> 131 us  [finish_views_on_mesh(): side_arr = jax.lax.ppermute(z2, 'fsdp', seen)]
    reduce_scatter x1, waiting for transfers between devices: 77.8 us -> 0.01 us  [local(): lax.psum_scatter(lax.dot_general(columns, cot_rows, (((0,), (0,)), ((), (...]
    all_gather x1 -> x0, waiting for transfers between devices: 41.6 us -> none  [local(): lax.all_gather(out_weight, 'fsdp', axis=0, tiled=True)]
    unnamed x9 -> x16, local copies, waits for them, and re-layouts: 3.22 us -> 12 us
    ppermute x0 -> x3, starting transfers between devices: none -> 5.48 us  [finish_views_on_mesh(): side_arr = jax.lax.ppermute(z2, 'fsdp', seen)]
    concatenate x0 -> x1, local copies, waits for them, and re-layouts: none -> 2.74 us  [finish_views_on_mesh(): return jnp.roll(z2, last * field_out, d_out)]
    psum x1, blocking collectives: 19.7 us -> 22.2 us  [local(): squares = lax.psum(jnp.sum(summed * summed), 'fsdp')]
  transfers between devices with their start and end apart: 3 -> 5, of which waited for: 3 -> 4; matrix products, arithmetic and copies ran while one was open for 0% -> 5% of each run, Pallas kernels for 0% -> 0%
where the time goes in v1:
time: 234 us
  waiting for transfers between devices  138 us (59%)
  blocking collectives  41.7 us (18%)
  local copies, waits for them, and re-layouts  16.5 us (7%)
  between operations  14.9 us (6%)
  matrix products  11.8 us (5%)
  starting transfers between devices  6.06 us (3%)
  other arithmetic  4.61 us (2%)
    ppermute x3, waiting for transfers between devices, finish_views_on_mesh(): side_arr = jax.lax.ppermute(z2, 'fsdp', seen)  131 us
    psum x1, blocking collectives, local(): squares = lax.psum(jnp.sum(summed * summed), 'fsdp')  22.2 us
    psum x1, blocking collectives, local(): summed = lax.psum(fsdp_summed, 'dp')  19.5 us
    unnamed x16, local copies, waits for them, and re-layouts  12 us
    ppermute x1, waiting for transfers between devices, from_behind(): lax.ppermute(shard, axis, [(i, (i + by) % size) for i in range(size)])  6.67 us
    ppermute x3, starting transfers between devices, finish_views_on_mesh(): side_arr = jax.lax.ppermute(z2, 'fsdp', seen)  5.48 us
  transfers between devices with their start and end apart: 5, of which 4 were waited for; matrix products, arithmetic and copies ran while one was open for 5% of the time, Pallas kernels for 0%

profile of v1, /device:TPU:0, one launch (start us, length us, event | category | flops | bytes accessed | tf_op | source)
XLA Modules:
  0.0 233.6 jit_solution(8576842461800839065)
XLA Ops:
  7.2 1.4 copy.21
  9.4 1.4 copy.19
  10.8 1.4 copy.20
  12.3 2.3 %fusion.26 = (f32[2,16,128]{2,1,0:T(8,128)S(1)}, f32[2,16,128,128]{2,3,1,0:T(8,128)}) fusion(pred[2,128]{1,0:T(4,128)(4,1)S(1)} %iota_compare_fusion, bf16[2,128,16,80]{1,3,2,0:T(8,128)(2,1)S(1)} %bitcast.25, bf16[2,128,16,80]{1,3,2,0:T(8,128)(2,1)S(1)} %bitcast.26), kind=kOutput, calls=%fused_computation.42 | convolution fusion | flops 85983360 | bytes 3424512 | tf_op jit(solution)/shard_map/sub | solution.py:28
  14.6 2.1 fusion.10
  16.7 1.0 copy.23
  17.7 0.8 convolution_convert_fusion.1
  19.9 6.7 %collective-permute-done = bf16[1,128,1280]{2,1,0:T(8,128)(2,1)S(1)} collective-permute-done((bf16[1,128,1280]{2,1,0:T(8,128)(2,1)S(1)}, bf16[1,128,1280]{2,1,0:T(8,128)(2,1)S(1)}, u32[]{:S(2)}, u32[]{:S(2)}) %collective-permute-start) | collective-permute-done | bytes 327712 | tf_op jit(solution)/shard_map/ppermute | solution.py:11
  27.3 2.8 %convolution_convert_fusion = bf16[1280,1280]{1,0:T(8,128)(2,1)} fusion(bf16[1,128,1280]{2,1,0:T(8,128)(2,1)S(1)} %copy-done, bf16[1,128,1280]{2,0,1:T(2,128)(2,1)S(1)} %slice_add_fusion), kind=kOutput, calls=%fused_computation.1 | convolution fusion | flops 421068800 | bytes 3932160 | tf_op jit(solution)/shard_map/dot_general | solution.py:84
  30.2 5.4 %collective-permute-start.1 = (bf16[160,1280]{1,0:T(8,128)(2,1)S(1)}, bf16[160,1280]{1,0:T(8,128)(2,1)S(1)}, u32[]{:S(2)}, u32[]{:S(2)}) collective-permute-start(bf16[160,1280]{1,0:T(8,128)(2,1)S(1)} %copy-done.1), channel_id=1, source_target_pairs={{0,7},{1,0},{2,1},{3,2},{4,3},{5,4},{6,5},{7,6},{8,15},{9,8},{10,9... | collective-permute-start | bytes 1228808 | tf_op jit(solution)/shard_map/ppermute | solution.py:63
  35.6 15.7 %collective-permute-done.1 = bf16[160,1280]{1,0:T(8,128)(2,1)S(1)} collective-permute-done((bf16[160,1280]{1,0:T(8,128)(2,1)S(1)}, bf16[160,1280]{1,0:T(8,128)(2,1)S(1)}, u32[]{:S(2)}, u32[]{:S(2)}) %collective-permute-start.1) | collective-permute-done | bytes 409632 | tf_op jit(solution)/shard_map/ppermute | solution.py:63
  51.4 35.4 %collective-permute-done.2 = bf16[320,1280]{1,0:T(8,128)(2,1)S(1)} collective-permute-done((bf16[320,1280]{1,0:T(8,128)(2,1)S(1)}, bf16[320,1280]{1,0:T(8,128)(2,1)S(1)}, u32[]{:S(2)}, u32[]{:S(2)}) %collective-permute-start.2) | collective-permute-done | bytes 819232 | tf_op jit(solution)/shard_map/ppermute | solution.py:63
  86.9 1.3 pad_maximum_fusion
  89.7 1.0 constant_dynamic-update-slice_fusion.5
  90.7 80.2 %collective-permute-done.3 = bf16[640,1280]{1,0:T(8,128)(2,1)} collective-permute-done((bf16[640,1280]{1,0:T(8,128)(2,1)}, bf16[640,1280]{1,0:T(8,128)(2,1)}, u32[]{:S(2)}, u32[]{:S(2)}) %collective-permute-start.3) | collective-permute-done | bytes 1638432 | tf_op jit(solution)/shard_map/ppermute | solution.py:63
  170.9 2.7 %constant_dynamic-update-slice_fusion.4 = bf16[2560,1280]{1,0:T(8,128)(2,1)} fusion(bf16[2560,1280]{1,0:T(8,128)(2,1)} %constant_dynamic-update-slice_fusion.5, bf16[640,1280]{1,0:T(8,128)(2,1)} %collective-permute-done.3), kind=kLoop, calls=%fused_computation.31 | loop fusion | bytes 3276800
  174.4 0.8 constant_dynamic-update-slice_fusion.2
  175.2 0.9 constant_dynamic-update-slice_fusion.1
  176.1 2.7 %constant_dynamic-update-slice_fusion = bf16[2560,1280]{1,0:T(8,128)(2,1)} fusion(bf16[2560,1280]{1,0:T(8,128)(2,1)} %constant_dynamic-update-slice_fusion.1, bf16[640,1280]{1,0:T(8,128)(2,1)} %collective-permute-done.3), kind=kLoop, calls=%fused_computation.27 | loop fusion | bytes 3276800 | tf_op jit(solution)/shard_map/jit(_roll_dynamic)/concatenate | solution.py:66
  178.9 19.5 %all-reduce.1 = f32[160,1280]{1,0:T(8,128)S(1)} all-reduce(bf16[160,1280]{1,0:T(8,128)(2,1)} %reduce-scatter.2.cloned.1.call-done), channel_id=1, replica_groups=mesh['dp'=4,'fsdp'=8] {'dp'}, use_global_device_ids=true, to_apply=%region_3.4 | all-reduce | flops 204800 | bytes 1228800 | tf_op jit(solution)/shard_map/psum | solution.py:91
  198.4 0.8 multiply_reduce_fusion
  199.2 3.7 %fusion.6 = bf16[1,128,1280]{2,1,0:T(8,128)(2,1)} fusion(bf16[2560,1280]{1,0:T(8,128)(2,1)} %constant_dynamic-update-slice_fusion, s32[]{:T(128)S(6)} %select_n.25, bf16[1,128,1280]{2,0,1:T(2,128)(2,1)S(1)} %slice_add_fusion), kind=kOutput, calls=%fused_computation.6 | convolution fusion | flops 419594240 | bytes 3932164 | tf_op jit(solution)/shard_map/dot_general | solution.py:77
  202.9 22.2 %psum.15 = f32[]{:T(128)} all-reduce(f32[]{:T(128)} %multiply_reduce_fusion), channel_id=1, replica_groups=mesh['dp'=4,'fsdp'=8] {'fsdp'}, use_global_device_ids=true, to_apply=%region_5.6 | all-reduce | flops 1 | bytes 8 | tf_op jit(solution)/shard_map/psum | solution.py:92
  225.8 0.9 broadcast_multiply_fusion
  (20 shorter events, 5.3 us)
Async XLA Ops:
  7.2 20.1 %copy-start = (bf16[1,128,1280]{2,1,0:T(8,128)(2,1)S(1)}, bf16[1,128,1280]{2,1,0:T(8,128)(2,1)}, u32[]{:S(2)}) copy-start(bf16[1,128,1280]{2,1,0:T(8,128)(2,1)} %param.12) | copy-start | bytes 983044
  7.2 171.7 %reduce-scatter.2.cloned.1.call-start = ((), (), s32[]{:S(2)}) async-start(), calls=%async_computation.1 | async-start | bytes 3686400 | tf_op jit(solution)/shard_map/reduce_scatter | solution.py:83
  14.6 3.1 %copy-start.2 = (s32[2]{0:T(128)S(1)}, s32[2]{0:T(128)}, u32[]{:S(2)}) copy-start(s32[2]{0:T(128)} %param.11) | copy-start | bytes 28
  19.3 7.2 %collective-permute-start = (bf16[1,128,1280]{2,1,0:T(8,128)(2,1)S(1)}, bf16[1,128,1280]{2,1,0:T(8,128)(2,1)S(1)}, u32[]{:S(2)}, u32[]{:S(2)}) collective-permute-start(bf16[1,128,1280]{2,1,0:T(8,128)(2,1)S(1)} %copy.24), channel_id=1, source_target_pairs={{0,8},{8,16},{16,24},{24,0},{1,9},{9,17},{17,25},{25,1},{2,10},{10... | collective-permute-start | bytes 983048 | tf_op jit(solution)/shard_map/ppermute | solution.py:11
  27.3 2.8 %copy-start.1 = (bf16[160,1280]{1,0:T(8,128)(2,1)S(1)}, bf16[160,1280]{1,0:T(8,128)(2,1)}, u32[]{:S(2)}) copy-start(bf16[160,1280]{1,0:T(8,128)(2,1)} %param.13) | copy-start | bytes 1228804
  30.2 21.2 %collective-permute-start.1 = (bf16[160,1280]{1,0:T(8,128)(2,1)S(1)}, bf16[160,1280]{1,0:T(8,128)(2,1)S(1)}, u32[]{:S(2)}, u32[]{:S(2)}) collective-permute-start(bf16[160,1280]{1,0:T(8,128)(2,1)S(1)} %copy-done.1), channel_id=1, source_target_pairs={{0,7},{1,0},{2,1},{3,2},{4,3},{5,4},{6,5},{7,6},{8,15},{9,8},{10,9... | collective-permute-start | bytes 1228808 | tf_op jit(solution)/shard_map/ppermute | solution.py:63
  51.4 35.5 %collective-permute-start.2 = (bf16[320,1280]{1,0:T(8,128)(2,1)S(1)}, bf16[320,1280]{1,0:T(8,128)(2,1)S(1)}, u32[]{:S(2)}, u32[]{:S(2)}) collective-permute-start(bf16[320,1280]{1,0:T(8,128)(2,1)S(1)} %pad_maximum_fusion.1), channel_id=1, source_target_pairs={{0,6},{1,7},{2,0},{3,1},{4,2},{5,3},{6,4},{7,5},{8,14},{9,15},{10,... | collective-permute-start | bytes 2457608 | tf_op jit(solution)/shard_map/ppermute | solution.py:63
  88.2 82.7 %collective-permute-start.3 = (bf16[640,1280]{1,0:T(8,128)(2,1)}, bf16[640,1280]{1,0:T(8,128)(2,1)}, u32[]{:S(2)}, u32[]{:S(2)}) collective-permute-start(bf16[640,1280]{1,0:T(8,128)(2,1)} %pad_maximum_fusion), channel_id=1, source_target_pairs={{0,4},{1,5},{2,6},{3,7},{4,0},{5,1},{6,2},{7,3},{8,12},{9,13},{10,... | collective-permute-start | bytes 4915208 | tf_op jit(solution)/shard_map/ppermute | solution.py:63
Sparse Core Ops, SparseCore 0:
  30.3 140.8 reduce-scatter.1
